TPU v7x, 512 devices: a whole 4x4x16 slice. The times are simulated.
512 devices in a mesh: freq: 64 (over y, x, z_hi, core), blk: 8 (over z_lo).
Axes of the slice: x: 4, y: 4, z: 16 (z_hi: 2, z_lo: 8; z = z_hi * 8 + z_lo), core: 2. Of those that a mesh axis runs over, the one named last changes fastest.
Arguments:
- samples: bfloat16 [1024, 267776], P(('blk', 'freq')), may hold values from -127 to 127, as said below
- slot_order: int32 [8, 128], P('blk'), may hold values from 0 to 127, each once within a row
- flags: int32 [1024], P(('blk', 'freq')), may hold values 0 or 1
Outputs:
- visibilities: float32 [256, 2, 1024, 1024], P('freq', None, 'blk')
Inputs may be any that keep to these rules, and one draw needn't show every extreme that they name: `samples`: every sample is a whole number.
All inputs are finite; a program needn't handle non-finite values. No bound on the sum of `flags` on one device may be relied on, other than what follows from the above.
Results may differ from a plain program's by a relative error of at most 0.0059.
Values may be sent and summed in bfloat16 or wider, within the bound.
A program may use at most 64 MiB of HBM per device.

v0:
```python
import math

import jax
import jax.numpy as jnp
from jax import lax
from jax.sharding import PartitionSpec as P

CH = 256
TAPS = 12
SPEC = 512


def prototype():
    count = TAPS * 2 * CH
    index = jnp.arange(count, dtype=jnp.float32)
    frame = 2.0 * CH
    shifted = (index + 0.5) / frame - TAPS / 2.0
    window = 0.5 - 0.5 * jnp.cos(2.0 * math.pi * (index + 0.5) / count)
    return (jnp.sinc(shifted) * window).astype(jnp.float32).reshape(TAPS, 2 * CH)


def twiddle():
    frame = 2 * CH
    chan = jnp.arange(CH, dtype=jnp.int32)[:, None]
    point = jnp.arange(frame, dtype=jnp.int32)[None, :]
    phase = (chan * point % frame).astype(jnp.float32) * (2.0 * math.pi / frame)
    table = jnp.stack([jnp.cos(phase), -jnp.sin(phase)], axis=1)
    return table.reshape(2 * CH, frame).astype(jnp.bfloat16)


def normalize(spectra, good):
    squares = jnp.sum(spectra * spectra, axis=2)
    power = jnp.sum(squares.reshape(spectra.shape[0] // 2, 2, squares.shape[1]), axis=1) / SPEC
    scale = good[None, :] / jnp.sqrt(power + 1e-05)
    return (spectra * jnp.repeat(scale, 2, axis=0)[:, :, None]).astype(jnp.bfloat16)


def make_tile(own, other):
    block = own.shape[1] // 2
    width = other.shape[1] // 2
    gram = jnp.einsum("cas,cbs->cab", own, other, preferred_element_type=jnp.float32)
    real_real = gram[:, :block, :width]
    real_imag = gram[:, :block, width:]
    imag_real = gram[:, block:, :width]
    imag_imag = gram[:, block:, width:]
    return jnp.stack([(real_real + imag_imag) / SPEC, (imag_real - real_imag) / SPEC], axis=1)


def body(samples, slot_order, flags):
    local_inputs = samples.shape[0]
    taps = prototype()
    table = twiddle()
    good = (1 - flags).astype(jnp.float32)
    frames = samples.reshape(local_inputs, SPEC + TAPS - 1, 2 * CH)
    total = jnp.zeros((local_inputs, SPEC, 2 * CH), jnp.float32)
    for tap in range(TAPS):
        total = total + taps[tap][None, None, :] * frames[:, tap : tap + SPEC, :].astype(
            jnp.float32
        )
    fir = total.astype(jnp.bfloat16)
    spectra = jnp.einsum("kn,isn->kis", table, fir, preferred_element_type=jnp.float32)
    masked = spectra * good[None, :, None]
    arrived = lax.all_to_all(masked, "freq", split_axis=0, concat_axis=1, tiled=True)
    moved = normalize(arrived, jnp.ones((arrived.shape[1],), jnp.float32))
    local_chans = moved.shape[0] // 2
    block = moved.shape[1]
    arranged = jnp.take(moved.reshape(local_chans, 2, block, SPEC), slot_order[0], axis=2)
    own = arranged.reshape(local_chans, 2 * block, SPEC)
    piece = lax.all_gather(arranged, "blk", axis=2, tiled=True)
    return make_tile(own, piece.reshape(local_chans, 2 * piece.shape[2], SPEC))


def solution(mesh):
    in_specs = (P(("blk", "freq"), None), P("blk", None), P(("blk", "freq")))
    out_specs = P("freq", None, "blk", None)
    return jax.shard_map(body, mesh=mesh, in_specs=in_specs, out_specs=out_specs, check_vma=False)
```

profile of v0, /device:TPU:1, one launch (start us, length us, event | category | flops | bytes accessed | tf_op | source)
XLA Modules:
  0.0 354.9 jit_solution(261696951317561511)
XLA Ops:
  6.5 0.0 copy-start.1
  6.5 2.2 negate_convert_fusion
  8.7 0.1 fusion.15
  8.9 0.1 pad_maximum_fusion.1
  8.9 0.5 copy.28
  9.5 0.2 reshape.173
  9.7 0.0 copy-done.1
  9.7 0.0 copy-done
  9.7 0.6 reshape.162
  10.4 3.5 convolution_multiply_fusion
  13.8 2.9 copy.29
  16.8 22.4 %all-to-all-start = ((f32[512,2,512]{2,1,0:T(2,128)}), f32[512,2,512]{2,1,0:T(2,128)S(1)}, u32[]{:S(2)}, u32[]{:S(2)}) async-start(f32[512,2,512]{2,1,0:T(2,128)} %copy.29), calls=%async_computation | async-start | bytes 4194304 | tf_op jit(solution)/shard_map/all_to_all | solution.py:63
  39.2 0.0 all-gather.2.cloned.1.call-start
  39.2 0.0 copy-done.2
  39.3 66.2 %all-to-all-done = f32[512,2,512]{2,1,0:T(2,128)S(1)} async-done(((f32[512,2,512]{2,1,0:T(2,128)}), f32[512,2,512]{2,1,0:T(2,128)S(1)}, u32[]{:S(2)}, u32[]{:S(2)}) %all-to-all-start) | async-done | bytes 2097184 | tf_op jit(solution)/shard_map/all_to_all | solution.py:63
  105.4 2.1 copy_bitcast_fusion
  107.5 3.7 %all_to_all.16 = f32[4,2,128,512]{3,2,1,0:T(8,128)} reshape(f32[8,64,2,512]{3,2,1,0:T(2,128)} %copy_bitcast_fusion) | data formatting | bytes 4194304 | tf_op jit(solution)/shard_map/all_to_all | solution.py:63
  111.2 0.9 multiply_reduce_fusion
  112.1 0.2 reshape.163
  112.3 0.1 copy.31
  112.4 3.0 fusion.4
  115.4 1.5 gather_fusion
  116.9 1.5 broadcast_select_fusion
  118.4 0.0 all-gather.2.cloned.1.call-update
  118.5 0.3 copy.33
  118.8 0.2 bitcast_select_fusion
  119.0 209.8 %all-gather.2.cloned.1.call-done = bf16[4,2,1024,512]{3,0,1,2:T(4,128)(2,1)} async-done(((bf16[4,2,128,512]{3,0,1,2:T(4,128)(2,1)}), bf16[4,2,1024,512]{3,0,1,2:T(4,128)(2,1)}) %all-gather.2.cloned.1.call-update) | async-done | bytes 8388624 | tf_op jit(solution)/shard_map/all_gather | solution.py:69
  328.8 9.5 %copy.34 = bf16[4,2,1024,512]{3,2,1,0:T(8,128)(2,1)} copy(bf16[4,2,1024,512]{3,0,1,2:T(4,128)(2,1)} %all-gather.2.cloned.1.call-done) | data formatting | bytes 16777216 | tf_op jit(solution)/shard_map/all_gather | solution.py:69
  338.2 5.8 %fusion.26 = f32[4,256,2048]{2,1,0:T(8,128)S(1)} fusion(bf16[4,256,512]{2,1,0:T(8,128)(2,1)S(1)} %bitcast_select_fusion, bf16[4,2048,512]{2,1,0:T(8,128)(2,1)} %bitcast.27), kind=kOutput, calls=%fused_computation.61 | convolution fusion | flops 2147483648 | bytes 17825792 | tf_op jit(solution)/shard_map/cas,cbs->cab/dot_general | solution.py:41
  344.0 1.4 fusion.3
  345.4 0.3 pad_maximum_fusion
  345.7 2.3 copy.35
  (10 shorter events, 0.1 us)
Async XLA Ops:
  6.5 3.1 copy-start.1
  6.5 3.2 copy-start
  16.8 22.4 %copy-start.2 = (s32[1,128]{1,0:T(1,128)S(1)}, s32[1,128]{1,0:T(1,128)}, u32[]{:S(2)}) copy-start(s32[1,128]{1,0:T(1,128)} %param.4) | copy-start | bytes 1540
  16.8 88.6 %all-to-all-start = ((f32[512,2,512]{2,1,0:T(2,128)}), f32[512,2,512]{2,1,0:T(2,128)S(1)}, u32[]{:S(2)}, u32[]{:S(2)}) async-start(f32[512,2,512]{2,1,0:T(2,128)} %copy.29), calls=%async_computation | async-start | bytes 4194304 | tf_op jit(solution)/shard_map/all_to_all | solution.py:63
  39.2 289.6 %all-gather.2.cloned.1.call-start = ((), (), s32[]{:S(2)}) async-start(), calls=%async_computation.1 | async-start | bytes 9437184 | tf_op jit(solution)/shard_map/all_gather | solution.py:69
Sparse Core Ops, SparseCore 0:
  118.6 210.1 all-gather.1
where the time goes:
time: 355 us
  waiting for transfers between devices  276 us (78%)
  local copies, waits for them, and re-layouts  24 us (7%)
  starting transfers between devices  22.4 us (6%)
  between operations  13.6 us (4%)
  other arithmetic  9.77 us (3%)
  matrix products  9.21 us (3%)
    all_gather x1, waiting for transfers between devices, body(): piece = lax.all_gather(arranged, 'blk', axis=2, tiled=True)  210 us
    all_to_all x1, waiting for transfers between devices, body(): lax.all_to_all(masked, 'freq', split_axis=0, concat_axis=1, tiled=True)  66.2 us
    all_to_all x1, starting transfers between devices, body(): lax.all_to_all(masked, 'freq', split_axis=0, concat_axis=1, tiled=True)  22.4 us
    all_gather x1, local copies, waits for them, and re-layouts, body(): piece = lax.all_gather(arranged, 'blk', axis=2, tiled=True)  9.46 us
  transfers between devices with their start and end apart: 2, of which 2 were waited for; matrix products, arithmetic and copies ran while one was open for 0% of the time, Pallas kernels for 0%

commit v1 on v0

v1 whole, which is shorter than its diff:
```python
import functools
import math

import jax
import jax.numpy as jnp
from jax import lax
from jax.experimental import pallas as pl
from jax.experimental.pallas import tpu as pltpu
from jax.sharding import PartitionSpec as P

CH = 256
TAPS = 12
SPEC = 512
MESH = pl.DeviceIdType.MESH


def prototype():
    count = TAPS * 2 * CH
    index = jnp.arange(count, dtype=jnp.float32)
    frame = 2.0 * CH
    shifted = (index + 0.5) / frame - TAPS / 2.0
    window = 0.5 - 0.5 * jnp.cos(2.0 * math.pi * (index + 0.5) / count)
    return (jnp.sinc(shifted) * window).astype(jnp.float32).reshape(TAPS, 2 * CH)


def twiddle():
    frame = 2 * CH
    chan = jnp.arange(CH, dtype=jnp.int32)[:, None]
    point = jnp.arange(frame, dtype=jnp.int32)[None, :]
    phase = (chan * point % frame).astype(jnp.float32) * (2.0 * math.pi / frame)
    table = jnp.stack([jnp.cos(phase), -jnp.sin(phase)], axis=1)
    return table.reshape(2 * CH, frame).astype(jnp.bfloat16)


def tile(rows, cols):
    half = rows.shape[0] // 2
    gram = lax.dot_general(rows, cols, (((1,), (1,)), ((), ())), preferred_element_type=jnp.float32)
    real = gram[:half, :half] + gram[half:, half:]
    imag = gram[half:, :half] - gram[:half, half:]
    return real * (1.0 / SPEC), imag * (1.0 / SPEC)


def correlate_kernel(n, own, out, rbuf, lbuf, tls, tlr, trs, trr,
                     rsend, rrecv, lsend, lrecv, tlsend, tlrecv, trsend, trrecv):
    me = lax.axis_index("blk")
    depth, chans, block = n // 2, own.shape[0], own.shape[1] // 2
    dr = depth - lax.rem(lax.axis_index("freq"), 2)
    dl = n - 1 - dr

    def right(t, c, src):
        return pltpu.make_async_remote_copy(
            src, rbuf.at[t, c], rsend.at[t, c], rrecv.at[t, c],
            device_id={"blk": lax.rem(me + 1, n)}, device_id_type=MESH)

    def left(t, c, src):
        return pltpu.make_async_remote_copy(
            src, lbuf.at[t, c], lsend.at[t, c], lrecv.at[t, c],
            device_id={"blk": lax.rem(me + n - 1, n)}, device_id_type=MESH)

    def tile_left(k, c):
        return pltpu.make_async_remote_copy(
            tls.at[k - 1, c], tlr.at[k - 1, c], tlsend.at[k - 1, c], tlrecv.at[k - 1, c],
            device_id={"blk": lax.rem(me + n - k, n)}, device_id_type=MESH)

    def tile_right(k, c):
        return pltpu.make_async_remote_copy(
            trs.at[k - 1, c], trr.at[k - 1, c], trsend.at[k - 1, c], trrecv.at[k - 1, c],
            device_id={"blk": lax.rem(me + k, n)}, device_id_type=MESH)

    def put(c, column, real, imag):
        at = pl.ds(pl.multiple_of(column * block, block), block)
        out[c, 0, :, at] = real.astype(jnp.float32)
        out[c, 1, :, at] = imag.astype(jnp.float32)

    barrier = pltpu.get_barrier_semaphore()
    for k in range(1, n):
        pl.semaphore_signal(barrier, 1, device_id={"blk": lax.rem(me + k, n)}, device_id_type=MESH)
    pl.semaphore_wait(barrier, n - 1)

    for c in range(chans):
        @pl.when(me < n - 1)
        def _():
            right(0, c, own.at[c]).start()

        @pl.when(me > 0)
        def _():
            left(0, c, own.at[c]).start()

    @pl.loop(0, chans)
    def _(c):
        put(c, me, *tile(own[c], own[c]))

    @pl.loop(0, depth)
    def _(t):
        from_left = (t < dr) & (me - 1 - t >= 0)
        from_right = (t < dl) & (me + 1 + t < n)

        @pl.loop(0, chans)
        def _(c):
            @pl.when(from_left)
            def _():
                right(t, c, own.at[c]).wait_recv()

                @pl.when((t + 1 < dr) & (me < n - 1))
                def _():
                    right(t + 1, c, rbuf.at[t, c]).start()

            @pl.when(from_right)
            def _():
                left(t, c, own.at[c]).wait_recv()

                @pl.when((t + 1 < dl) & (me > 0))
                def _():
                    left(t + 1, c, lbuf.at[t, c]).start()

            @pl.loop(1, depth + 1)
            def _(k):
                @pl.when((me + dl < n) & (me - k >= 0) & (k <= dr) & (jnp.maximum(k, dl) == t + 1))
                def _():
                    real, imag = tile(rbuf[k - 1, c], lbuf[dl - 1, c])
                    tls[k - 1, c, 0] = real.astype(jnp.bfloat16)
                    tls[k - 1, c, 1] = imag.astype(jnp.bfloat16)
                    tile_left(k, c).start()

                @pl.when((me - dr >= 0) & (me + k < n) & (k <= dl) & (jnp.maximum(k, dr) == t + 1))
                def _():
                    real, imag = tile(lbuf[k - 1, c], rbuf[dr - 1, c])
                    trs[k - 1, c, 0] = real.astype(jnp.bfloat16)
                    trs[k - 1, c, 1] = imag.astype(jnp.bfloat16)
                    tile_right(k, c).start()

            @pl.when(from_left)
            def _():
                put(c, me - 1 - t, *tile(own[c], rbuf[t, c]))

            @pl.when(from_right)
            def _():
                put(c, me + 1 + t, *tile(own[c], lbuf[t, c]))

    @pl.loop(0, chans)
    def _(c):
        @pl.loop(1, depth + 1)
        def _(k):
            @pl.when((me + k + dl < n) & (k <= dr))
            def _():
                tile_left(k, c).wait_recv()
                put(c, me + k + dl, tlr[k - 1, c, 0], tlr[k - 1, c, 1])

            @pl.when((me - k - dr >= 0) & (k <= dl))
            def _():
                tile_right(k, c).wait_recv()
                put(c, me - k - dr, trr[k - 1, c, 0], trr[k - 1, c, 1])

    @pl.loop(0, chans)
    def _(c):
        @pl.loop(0, depth)
        def _(t):
            @pl.when((t < dr) & (me - t >= 0) & (me < n - 1))
            def _():
                right(t, c, own.at[c]).wait_send()

            @pl.when((t < dl) & (me + t < n) & (me > 0))
            def _():
                left(t, c, own.at[c]).wait_send()

            @pl.when((me + dl < n) & (me - t - 1 >= 0) & (t + 1 <= dr))
            def _():
                tile_left(t + 1, c).wait_send()

            @pl.when((me - dr >= 0) & (me + t + 1 < n) & (t + 1 <= dl))
            def _():
                tile_right(t + 1, c).wait_send()


def correlate(n, own):
    chans, rows, spec = own.shape
    depth, block = n // 2, rows // 2
    held = pltpu.VMEM((depth, chans, rows, spec), jnp.bfloat16)
    tiles = pltpu.VMEM((depth, chans, 2, block, block), jnp.bfloat16)
    sems = pltpu.SemaphoreType.DMA((depth, chans))
    return pl.pallas_call(
        functools.partial(correlate_kernel, n),
        out_shape=jax.ShapeDtypeStruct((chans, 2, block, n * block), jnp.float32),
        in_specs=[pl.BlockSpec(memory_space=pltpu.VMEM)],
        out_specs=pl.BlockSpec(memory_space=pltpu.VMEM),
        scratch_shapes=[held, held, tiles, tiles, tiles, tiles] + [sems] * 8,
        compiler_params=pltpu.CompilerParams(
            collective_id=0, has_side_effects=True, vmem_limit_bytes=48 << 20),
    )(own)


def body(n, samples, slot_order, flags):
    inputs = samples.shape[0]
    taps = prototype()
    table = twiddle()
    good = (1 - flags).astype(jnp.float32)
    frames = samples.reshape(inputs, SPEC + TAPS - 1, 2 * CH)
    total = jnp.zeros((inputs, SPEC, 2 * CH), jnp.float32)
    for tap in range(TAPS):
        total = total + taps[tap][None, None, :] * frames[:, tap : tap + SPEC, :].astype(jnp.float32)
    fir = total.astype(jnp.bfloat16)
    spectra = jnp.einsum("kn,isn->iks", table, fir, preferred_element_type=jnp.float32)
    squares = jnp.sum(spectra * spectra, axis=2)
    power = jnp.sum(squares.reshape(inputs, CH, 2), axis=2) / SPEC
    scale = good[:, None] / jnp.sqrt(power + 1e-05)
    quantized = (spectra * jnp.repeat(scale, 2, axis=1)[:, :, None]).astype(jnp.bfloat16)

    groups = lax.axis_size("freq")
    rows = 2 * CH // groups
    leaving = quantized.reshape(inputs, groups, rows, SPEC).transpose(1, 0, 2, 3)
    arrived = lax.all_to_all(leaving.reshape(groups, inputs * rows, SPEC), "freq", 0, 0, tiled=True)
    block = groups * inputs
    arranged = jnp.take(arrived.reshape(block, rows, SPEC), slot_order[0], axis=0)
    own = arranged.transpose(1, 0, 2).reshape(rows // 2, 2 * block, SPEC)
    return correlate(n, own)


def solution(mesh):
    in_specs = (P(("blk", "freq"), None), P("blk", None), P(("blk", "freq")))
    out_specs = P("freq", None, "blk", None)
    return jax.shard_map(
        functools.partial(body, mesh.shape["blk"]), mesh=mesh, in_specs=in_specs, out_specs=out_specs, check_vma=False)
```

time: 355 us -> 212 us (0.60)
  waiting for transfers between devices: 276 us -> 32.1 us
  Pallas kernels: 0 us -> 142 us
  local copies, waits for them, and re-layouts: 24 us -> 5.69 us
  between operations: 13.6 us -> 0.12 us
  other arithmetic: 9.77 us -> 4.64 us
  matrix products: 9.21 us -> 4.63 us
    all_gather x1 -> x0, waiting for transfers between devices: 210 us -> none  [body(): piece = lax.all_gather(arranged, 'blk', axis=2, tiled=True)]
    pallas_call x0 -> x1, Pallas kernels: none -> 142 us  [correlate(): pl.pallas_call(functools.partial(correlate_kernel, n), out_shape=jax.Shap...]
    all_to_all x1, waiting for transfers between devices: 66.2 us -> 32.1 us  [body(): lax.all_to_all(leaving.reshape(groups, inputs * rows, SPEC), 'freq', 0, 0...]
    all_gather x1 -> x0, local copies, waits for them, and re-layouts: 9.46 us -> none  [body(): piece = lax.all_gather(arranged, 'blk', axis=2, tiled=True)]
    all_to_all x2 -> x0, local copies, waits for them, and re-layouts: 5.78 us -> none  [body(): lax.all_to_all(masked, 'freq', split_axis=0, concat_axis=1, tiled=True)]
    dot_general x2 -> x1, matrix products: 9.21 us -> 4.63 us  [body(): jnp.einsum('kn,isn->iks', table, fir, preferred_element_type=jnp.float32)]
  transfers between devices with their start and end apart: 2 -> 1, of which waited for: 2 -> 1; matrix products, arithmetic and copies ran while one was open for 0% -> 0% of each run, Pallas kernels for 0% -> 0%
where the time goes in v1:
time: 212 us; the launch traced here: 211 us
  Pallas kernels  142 us (67%)
  waiting for transfers between devices  32.1 us (15%)
  starting transfers between devices  22.2 us (10%)
  local copies, waits for them, and re-layouts  5.69 us (3%)
  other arithmetic  4.64 us (2%)
  matrix products  4.63 us (2%)
    pallas_call x1, Pallas kernels, correlate(): pl.pallas_call(functools.partial(correlate_kernel, n), out_shape=jax.Shap...  142 us
    all_to_all x1, waiting for transfers between devices, body(): lax.all_to_all(leaving.reshape(groups, inputs * rows, SPEC), 'freq', 0, 0...  32.1 us
    all_to_all x1, starting transfers between devices, body(): lax.all_to_all(leaving.reshape(groups, inputs * rows, SPEC), 'freq', 0, 0...  22.2 us
    dot_general x1, matrix products, body(): jnp.einsum('kn,isn->iks', table, fir, preferred_element_type=jnp.float32)  4.63 us
  transfers between devices with their start and end apart: 1, of which 1 were waited for; matrix products, arithmetic and copies ran while one was open for 0% of the time, Pallas kernels for 0%

profile of v1, /device:TPU:1, one launch (start us, length us, event | category | flops | bytes accessed | tf_op | source)
XLA Modules:
  0.0 211.3 jit_solution(175696562506567394)
XLA Ops:
  0.0 0.0 copy-start
  0.0 0.1 fusion.12
  0.1 2.2 %negate_convert_fusion = (bf16[256,1,512]{2,0,1:T(8,128)(2,1)S(1)}, bf16[256,1,512]{2,0,1:T(8,128)(2,1)S(1)}) fusion(), kind=kLoop, calls=%fused_computation.15 | loop fusion | flops 2228224 | bytes 524288 | tf_op jit(solution)/shard_map/convert.1
  2.3 0.7 subtract_convert_fusion
  3.0 0.1 pad_maximum_fusion
  3.0 0.5 copy.8
  3.6 1.0 reshape.176
  4.6 0.0 copy-done
  4.6 0.6 reshape.162
  5.2 4.6 %multiply_reduce_fusion = (f32[2,512]{1,0:T(2,128)S(1)}, f32[2,512,512]{1,2,0:T(8,128)S(1)}) fusion(bf16[512,512,1]{1,0,2:T(8,128)(2,1)} %reshape.176, bf16[2,523,512]{2,1,0:T(8,128)(2,1)S(1)} %reshape.162, f32[512]{0:T(512)S(1)} %get-tuple-element.6, f32[512]{0:T(512)S(1)} %get-tuple-element.7, f32[512]{0:T(512)S(1)} %get-tuple-element.8, ...), kind=kOutput, calls=%fused_computation.2 | convolution fusion | flops 556792832 | bytes 15233024 | tf_op jit(solution)/shard_map/kn,isn->iks/dot_general | solution.py:202
  9.9 0.2 reshape.163
  10.1 0.1 reduce_sum.19
  10.2 0.1 rsqrt_multiply_fusion
  10.3 0.1 broadcast_in_dim.22
  10.4 0.2 mul.526
  10.6 0.0 copy-start.1
  10.6 1.2 copy_bitcast_fusion
  11.8 22.2 %all-to-all-start = ((bf16[64,16,512]{2,1,0:T(8,128)(2,1)}), bf16[64,16,512]{2,1,0:T(8,128)(2,1)S(1)}, u32[]{:S(2)}, u32[]{:S(2)}) async-start(bf16[64,16,512]{2,1,0:T(8,128)(2,1)} %copy_bitcast_fusion), calls=%async_computation | async-start | bytes 2097152 | tf_op jit(solution)/shard_map/all_to_all | solution.py:211
  34.1 0.0 copy-done.1
  34.1 32.1 %all-to-all-done = bf16[64,16,512]{2,1,0:T(8,128)(2,1)S(1)} async-done(((bf16[64,16,512]{2,1,0:T(8,128)(2,1)}), bf16[64,16,512]{2,1,0:T(8,128)(2,1)S(1)}, u32[]{:S(2)}, u32[]{:S(2)}) %all-to-all-start) | async-done | bytes 1048608 | tf_op jit(solution)/shard_map/all_to_all | solution.py:211
  66.2 0.6 gather_fusion
  66.9 0.2 select_bitcast_fusion
  67.1 0.3 copy.10
  67.4 141.9 %shard_map.37 = f32[4,2,128,1024]{3,2,1,0:T(8,128)S(1)} custom-call(bf16[4,256,512]{2,1,0:T(8,128)(2,1)S(1)} %bitcast.20), custom_call_target="tpu_custom_call" | custom-call | tf_op jit(solution)/shard_map/pallas_call | solution.py:181
  209.3 2.0 copy.13
  (4 shorter events, 0.0 us)
Async XLA Ops:
  0.0 4.6 %copy-start = (bf16[2,267776]{1,0:T(2,128)(2,1)S(1)}, bf16[2,267776]{1,0:T(2,128)(2,1)}, u32[]{:S(2)}) copy-start(bf16[2,267776]{1,0:T(2,128)(2,1)} %param.3) | copy-start | bytes 3213316
  10.6 23.4 %copy-start.1 = (s32[1,128]{1,0:T(1,128)S(1)}, s32[1,128]{1,0:T(1,128)}, u32[]{:S(2)}) copy-start(s32[1,128]{1,0:T(1,128)} %param.4) | copy-start | bytes 1540
  11.8 54.4 %all-to-all-start = ((bf16[64,16,512]{2,1,0:T(8,128)(2,1)}), bf16[64,16,512]{2,1,0:T(8,128)(2,1)S(1)}, u32[]{:S(2)}, u32[]{:S(2)}) async-start(bf16[64,16,512]{2,1,0:T(8,128)(2,1)} %copy_bitcast_fusion), calls=%async_computation | async-start | bytes 2097152 | tf_op jit(solution)/shard_map/all_to_all | solution.py:211

commit v2 on v1

v2 whole, which is shorter than its diff:
```python
import functools
import math

import jax
import jax.numpy as jnp
from jax import lax
from jax.experimental import pallas as pl
from jax.experimental.pallas import tpu as pltpu
from jax.sharding import PartitionSpec as P

CH = 256
TAPS = 12
SPEC = 512
MESH = pl.DeviceIdType.MESH


def prototype():
    count = TAPS * 2 * CH
    index = jnp.arange(count, dtype=jnp.float32)
    frame = 2.0 * CH
    shifted = (index + 0.5) / frame - TAPS / 2.0
    window = 0.5 - 0.5 * jnp.cos(2.0 * math.pi * (index + 0.5) / count)
    return (jnp.sinc(shifted) * window).astype(jnp.float32).reshape(TAPS, 2 * CH)


def twiddle():
    frame = 2 * CH
    chan = jnp.arange(CH, dtype=jnp.int32)[:, None]
    point = jnp.arange(frame, dtype=jnp.int32)[None, :]
    phase = (chan * point % frame).astype(jnp.float32) * (2.0 * math.pi / frame)
    table = jnp.stack([jnp.cos(phase), -jnp.sin(phase)], axis=1)
    return table.reshape(2 * CH, frame).astype(jnp.bfloat16)


def tile(rows, cols):
    half = rows.shape[0] // 2
    gram = lax.dot_general(rows, cols, (((1,), (1,)), ((), ())), preferred_element_type=jnp.float32)
    real = gram[:half, :half] + gram[half:, half:]
    imag = gram[half:, :half] - gram[:half, half:]
    return real * (1.0 / SPEC), imag * (1.0 / SPEC)


def correlate_kernel(n, own, out, nbuf, fbuf, ts, tr, nsend, nrecv, frecv, tsend, trecv):
    me = lax.axis_index("blk")
    half, chans, block = n // 2, own.shape[0], own.shape[1] // 2
    mid = half - 1
    side = me // half
    step = 1 - 2 * side
    place = me * step + (n - 1) * side
    inner = {"blk": me + step}

    def pass_near(t, c, src):
        return pltpu.make_async_remote_copy(
            src, nbuf.at[t, c], nsend.at[t, c], nrecv.at[t, c], device_id=inner, device_id_type=MESH)

    def pass_far(t, c, src):
        return pltpu.make_async_remote_copy(
            src, fbuf.at[t, c], nsend.at[t, c], frecv.at[t, c], device_id=inner, device_id_type=MESH)

    def give(t, v, slot, c):
        return pltpu.make_async_remote_copy(
            ts.at[t, v, c], tr.at[slot, c], tsend.at[t, v, c], trecv.at[slot, c],
            device_id={"blk": lax.rem(me - (t + 1) * step + n, n)}, device_id_type=MESH)

    def start(t, c, src):
        @pl.when(place < mid)
        def _():
            pass_near(t, c, src).start()

        @pl.when(place == mid)
        def _():
            pass_far(t, c, src).start()

    def put(c, column, real, imag):
        at = pl.ds(pl.multiple_of(column * block, block), block)
        out[c, 0, :, at] = real.astype(jnp.float32)
        out[c, 1, :, at] = imag.astype(jnp.float32)

    def relay(t, v, slot, c, rows, cols):
        real, imag = tile(rows, cols)
        ts[t, v, c, 0] = real.astype(jnp.bfloat16)
        ts[t, v, c, 1] = imag.astype(jnp.bfloat16)
        give(t, v, slot, c).start()

    barrier = pltpu.get_barrier_semaphore()
    for k in range(1, n):
        pl.semaphore_signal(barrier, 1, device_id={"blk": lax.rem(me + k, n)}, device_id_type=MESH)
    pl.semaphore_wait(barrier, n - 1)

    for c in range(chans):
        start(0, c, own.at[c])

    @pl.loop(0, chans)
    def _(c):
        put(c, me, *tile(own[c], own[c]))

    @pl.loop(0, half)
    def _(t):
        @pl.loop(0, chans)
        def _(c):
            @pl.when(t < place)
            def _():
                pass_near(t, c, own.at[c]).wait_recv()
                start(t + 1, c, nbuf.at[t, c])

            @pl.when(place == mid)
            def _():
                pass_far(t, c, own.at[c]).wait_recv()

            @pl.when(t < place)
            def _():
                relay(t, 0, place, c, nbuf[t, c], own[c])

            @pl.when(place == mid)
            def _():
                @pl.loop(0, mid)
                def _(r):
                    @pl.when(r <= t)
                    def _():
                        relay(r, 1 + t, half + t, c, nbuf[r, c], fbuf[t, c])

                @pl.when(t < mid)
                def _():
                    @pl.loop(0, mid)
                    def _(u):
                        @pl.when(u < t)
                        def _():
                            relay(t, 1 + u, half + u, c, nbuf[t, c], fbuf[u, c])

                put(c, me + (t + 1) * step, *tile(own[c], fbuf[t, c]))

            @pl.when(t < place)
            def _():
                put(c, me - (t + 1) * step, *tile(own[c], nbuf[t, c]))

    @pl.when(place < mid)
    def _():
        @pl.loop(0, n)
        def _(slot):
            @pl.when(slot > place)
            def _():
                @pl.loop(0, chans)
                def _(c):
                    give(0, 0, slot, c).wait_recv()
                    put(c, me + (slot - place) * step, tr[slot, c, 0], tr[slot, c, 1])

    @pl.loop(0, chans)
    def _(c):
        @pl.loop(0, half)
        def _(t):
            @pl.when(t <= place)
            def _():
                pass_far(t, c, own.at[c]).wait_send()

            @pl.when(t < place)
            def _():
                give(t, 0, 0, c).wait_send()

            @pl.when((place == mid) & (t < mid))
            def _():
                @pl.loop(1, half + 1)
                def _(v):
                    give(t, v, 0, c).wait_send()


def correlate(n, own):
    chans, rows, spec = own.shape
    half, block = n // 2, rows // 2
    near = pltpu.VMEM((half - 1, chans, rows, spec), jnp.bfloat16)
    far = pltpu.VMEM((half, chans, rows, spec), jnp.bfloat16)
    leaving = pltpu.VMEM((half - 1, half + 1, chans, 2, block, block), jnp.bfloat16)
    arriving = pltpu.VMEM((n, chans, 2, block, block), jnp.bfloat16)
    dma = pltpu.SemaphoreType.DMA
    return pl.pallas_call(
        functools.partial(correlate_kernel, n),
        out_shape=jax.ShapeDtypeStruct((chans, 2, block, n * block), jnp.float32),
        in_specs=[pl.BlockSpec(memory_space=pltpu.VMEM)],
        out_specs=pl.BlockSpec(memory_space=pltpu.VMEM),
        scratch_shapes=[
            near, far, leaving, arriving, dma((half, chans)), dma((half - 1, chans)), dma((half, chans)),
            dma((half - 1, half + 1, chans)), dma((n, chans))],
        compiler_params=pltpu.CompilerParams(
            collective_id=0, has_side_effects=True, vmem_limit_bytes=48 << 20),
    )(own)


def body(n, samples, slot_order, flags):
    inputs = samples.shape[0]
    taps = prototype()
    table = twiddle()
    good = (1 - flags).astype(jnp.float32)
    frames = samples.reshape(inputs, SPEC + TAPS - 1, 2 * CH)
    total = jnp.zeros((inputs, SPEC, 2 * CH), jnp.float32)
    for tap in range(TAPS):
        total = total + taps[tap][None, None, :] * frames[:, tap : tap + SPEC, :].astype(jnp.float32)
    fir = total.astype(jnp.bfloat16)
    spectra = jnp.einsum("kn,isn->iks", table, fir, preferred_element_type=jnp.float32)
    squares = jnp.sum(spectra * spectra, axis=2)
    power = jnp.sum(squares.reshape(inputs, CH, 2), axis=2) / SPEC
    scale = good[:, None] / jnp.sqrt(power + 1e-05)
    quantized = (spectra * jnp.repeat(scale, 2, axis=1)[:, :, None]).astype(jnp.bfloat16)

    groups = lax.axis_size("freq")
    rows = 2 * CH // groups
    leaving = quantized.reshape(inputs, groups, rows, SPEC).transpose(1, 0, 2, 3)
    arrived = lax.all_to_all(leaving.reshape(groups, inputs * rows, SPEC), "freq", 0, 0, tiled=True)
    block = groups * inputs
    arranged = jnp.take(arrived.reshape(block, rows, SPEC), slot_order[0], axis=0)
    own = arranged.transpose(1, 0, 2).reshape(rows // 2, 2 * block, SPEC)
    return correlate(n, own)


def solution(mesh):
    in_specs = (P(("blk", "freq"), None), P("blk", None), P(("blk", "freq")))
    out_specs = P("freq", None, "blk", None)
    return jax.shard_map(
        functools.partial(body, mesh.shape["blk"]), mesh=mesh, in_specs=in_specs, out_specs=out_specs, check_vma=False)
```

time: 212 us -> 207 us (0.976)
  Pallas kernels: 142 us -> 136 us
    pallas_call x1, Pallas kernels: 142 us -> 136 us  [correlate(): pl.pallas_call(functools.partial(correlate_kernel, n), out_shape=jax.Shap...]
where the time goes in v2:
time: 207 us; the launch traced here: 206 us
  Pallas kernels  136 us (66%)
  waiting for transfers between devices  32.1 us (16%)
  starting transfers between devices  22.2 us (11%)
  local copies, waits for them, and re-layouts  5.69 us (3%)
  other arithmetic  4.64 us (2%)
  matrix products  4.63 us (2%)
    pallas_call x1, Pallas kernels, correlate(): pl.pallas_call(functools.partial(correlate_kernel, n), out_shape=jax.Shap...  136 us
    all_to_all x1, waiting for transfers between devices, body(): lax.all_to_all(leaving.reshape(groups, inputs * rows, SPEC), 'freq', 0, 0...  32.1 us
    all_to_all x1, starting transfers between devices, body(): lax.all_to_all(leaving.reshape(groups, inputs * rows, SPEC), 'freq', 0, 0...  22.2 us
    dot_general x1, matrix products, body(): jnp.einsum('kn,isn->iks', table, fir, preferred_element_type=jnp.float32)  4.63 us
  transfers between devices with their start and end apart: 1, of which 1 were waited for; matrix products, arithmetic and copies ran while one was open for 0% of the time, Pallas kernels for 0%

profile of v2, /device:TPU:1, one launch (start us, length us, event | category | flops | bytes accessed | tf_op | source)
XLA Modules:
  0.0 205.7 jit_solution(2230748066925521612)
XLA Ops:
  0.0 0.0 copy-start
  0.0 0.1 fusion.12
  0.1 2.2 %negate_convert_fusion = (bf16[256,1,512]{2,0,1:T(8,128)(2,1)S(1)}, bf16[256,1,512]{2,0,1:T(8,128)(2,1)S(1)}) fusion(), kind=kLoop, calls=%fused_computation.15 | loop fusion | flops 2228224 | bytes 524288 | tf_op jit(solution)/shard_map/convert.1
  2.3 0.7 subtract_convert_fusion
  3.0 0.1 pad_maximum_fusion
  3.0 0.5 copy.8
  3.6 1.0 reshape.176
  4.6 0.0 copy-done
  4.6 0.6 reshape.162
  5.2 4.6 %multiply_reduce_fusion = (f32[2,512]{1,0:T(2,128)S(1)}, f32[2,512,512]{1,2,0:T(8,128)S(1)}) fusion(bf16[512,512,1]{1,0,2:T(8,128)(2,1)} %reshape.176, bf16[2,523,512]{2,1,0:T(8,128)(2,1)S(1)} %reshape.162, f32[512]{0:T(512)S(1)} %get-tuple-element.6, f32[512]{0:T(512)S(1)} %get-tuple-element.7, f32[512]{0:T(512)S(1)} %get-tuple-element.8, ...), kind=kOutput, calls=%fused_computation.2 | convolution fusion | flops 556792832 | bytes 15233024 | tf_op jit(solution)/shard_map/kn,isn->iks/dot_general | solution.py:197
  9.9 0.2 reshape.163
  10.1 0.1 reduce_sum.19
  10.2 0.1 rsqrt_multiply_fusion
  10.3 0.1 broadcast_in_dim.22
  10.4 0.2 mul.526
  10.6 0.0 copy-start.1
  10.6 1.2 copy_bitcast_fusion
  11.8 22.2 %all-to-all-start = ((bf16[64,16,512]{2,1,0:T(8,128)(2,1)}), bf16[64,16,512]{2,1,0:T(8,128)(2,1)S(1)}, u32[]{:S(2)}, u32[]{:S(2)}) async-start(bf16[64,16,512]{2,1,0:T(8,128)(2,1)} %copy_bitcast_fusion), calls=%async_computation | async-start | bytes 2097152 | tf_op jit(solution)/shard_map/all_to_all | solution.py:206
  34.1 0.0 copy-done.1
  34.1 32.1 %all-to-all-done = bf16[64,16,512]{2,1,0:T(8,128)(2,1)S(1)} async-done(((bf16[64,16,512]{2,1,0:T(8,128)(2,1)}), bf16[64,16,512]{2,1,0:T(8,128)(2,1)S(1)}, u32[]{:S(2)}, u32[]{:S(2)}) %all-to-all-start) | async-done | bytes 1048608 | tf_op jit(solution)/shard_map/all_to_all | solution.py:206
  66.2 0.6 gather_fusion
  66.9 0.2 select_bitcast_fusion
  67.1 0.3 copy.10
  67.4 136.3 %shard_map.37 = f32[4,2,128,1024]{3,2,1,0:T(8,128)S(1)} custom-call(bf16[4,256,512]{2,1,0:T(8,128)(2,1)S(1)} %bitcast.20), custom_call_target="tpu_custom_call" | custom-call | tf_op jit(solution)/shard_map/pallas_call | solution.py:174
  203.7 2.0 copy.13
  (4 shorter events, 0.0 us)
Async XLA Ops:
  0.0 4.6 %copy-start = (bf16[2,267776]{1,0:T(2,128)(2,1)S(1)}, bf16[2,267776]{1,0:T(2,128)(2,1)}, u32[]{:S(2)}) copy-start(bf16[2,267776]{1,0:T(2,128)(2,1)} %param.3) | copy-start | bytes 3213316
  10.6 23.4 %copy-start.1 = (s32[1,128]{1,0:T(1,128)S(1)}, s32[1,128]{1,0:T(1,128)}, u32[]{:S(2)}) copy-start(s32[1,128]{1,0:T(1,128)} %param.4) | copy-start | bytes 1540
  11.8 54.4 %all-to-all-start = ((bf16[64,16,512]{2,1,0:T(8,128)(2,1)}), bf16[64,16,512]{2,1,0:T(8,128)(2,1)S(1)}, u32[]{:S(2)}, u32[]{:S(2)}) async-start(bf16[64,16,512]{2,1,0:T(8,128)(2,1)} %copy_bitcast_fusion), calls=%async_computation | async-start | bytes 2097152 | tf_op jit(solution)/shard_map/all_to_all | solution.py:206

commit v3 on v2

--- a/solution.py
+++ b/solution.py
@@ -40,7 +40,7 @@
     return real * (1.0 / SPEC), imag * (1.0 / SPEC)
 
 
-def correlate_kernel(n, own, out, nbuf, fbuf, ts, tr, nsend, nrecv, frecv, tsend, trecv):
+def correlate_kernel(n, keep, swap, place_keep, place_swap, out, own, xbuf, xsend, xrecv, nbuf, fbuf, ts, tr, nsend, nrecv, frecv, tsend, trecv):
     me = lax.axis_index("blk")
     half, chans, block = n // 2, own.shape[0], own.shape[1] // 2
     mid = half - 1
@@ -82,16 +82,35 @@
         ts[t, v, c, 1] = imag.astype(jnp.bfloat16)
         give(t, v, slot, c).start()
 
+    group = lax.axis_index("freq")
+    partner = {"freq": group + 2 - 4 * lax.rem(group // 2, 2)}
+
+    def exchange(c):
+        return pltpu.make_async_remote_copy(
+            swap.at[c], xbuf.at[c], xsend.at[c], xrecv.at[c], device_id=partner, device_id_type=MESH)
+
     barrier = pltpu.get_barrier_semaphore()
     for k in range(1, n):
         pl.semaphore_signal(barrier, 1, device_id={"blk": lax.rem(me + k, n)}, device_id_type=MESH)
-    pl.semaphore_wait(barrier, n - 1)
+    pl.semaphore_signal(barrier, 1, device_id=partner, device_id_type=MESH)
+    pl.semaphore_wait(barrier, n)
 
     for c in range(chans):
-        start(0, c, own.at[c])
+        exchange(c).start()
 
     @pl.loop(0, chans)
     def _(c):
+        exchange(c).wait_recv()
+        for p in range(2):
+            rows = pl.ds(p * (block // 2), block // 2)
+            mixed = jnp.dot(place_keep[...], keep[c, rows, :], preferred_element_type=jnp.float32)
+            mixed += jnp.dot(place_swap[...], xbuf[c, rows, :], preferred_element_type=jnp.float32)
+            own[c, pl.ds(p * block, block), :] = mixed.astype(jnp.bfloat16)
+        start(0, c, own.at[c])
+
+    @pl.loop(0, chans)
+    def _(c):
+        exchange(c).wait_send()
         put(c, me, *tile(own[c], own[c]))
 
     @pl.loop(0, half)
@@ -163,9 +182,10 @@
                     give(t, v, 0, c).wait_send()
 
 
-def correlate(n, own):
-    chans, rows, spec = own.shape
-    half, block = n // 2, rows // 2
+def correlate(n, keep, swap, place_keep, place_swap):
+    chans, block, spec = keep.shape
+    half, rows = n // 2, 2 * block
+    own = pltpu.VMEM((chans, rows, spec), jnp.bfloat16)
     near = pltpu.VMEM((half - 1, chans, rows, spec), jnp.bfloat16)
     far = pltpu.VMEM((half, chans, rows, spec), jnp.bfloat16)
     leaving = pltpu.VMEM((half - 1, half + 1, chans, 2, block, block), jnp.bfloat16)
@@ -174,14 +194,15 @@
     return pl.pallas_call(
         functools.partial(correlate_kernel, n),
         out_shape=jax.ShapeDtypeStruct((chans, 2, block, n * block), jnp.float32),
-        in_specs=[pl.BlockSpec(memory_space=pltpu.VMEM)],
+        in_specs=[pl.BlockSpec(memory_space=pltpu.VMEM)] * 4,
         out_specs=pl.BlockSpec(memory_space=pltpu.VMEM),
         scratch_shapes=[
+            own, pltpu.VMEM(keep.shape, jnp.bfloat16), dma((chans,)), dma((chans,)),
             near, far, leaving, arriving, dma((half, chans)), dma((half - 1, chans)), dma((half, chans)),
             dma((half - 1, half + 1, chans)), dma((n, chans))],
         compiler_params=pltpu.CompilerParams(
             collective_id=0, has_side_effects=True, vmem_limit_bytes=48 << 20),
-    )(own)
+    )(keep, swap, place_keep, place_swap)
 
 
 def body(n, samples, slot_order, flags):
@@ -201,13 +222,24 @@
     quantized = (spectra * jnp.repeat(scale, 2, axis=1)[:, :, None]).astype(jnp.bfloat16)
 
     groups = lax.axis_size("freq")
-    rows = 2 * CH // groups
-    leaving = quantized.reshape(inputs, groups, rows, SPEC).transpose(1, 0, 2, 3)
-    arrived = lax.all_to_all(leaving.reshape(groups, inputs * rows, SPEC), "freq", 0, 0, tiled=True)
-    block = groups * inputs
-    arranged = jnp.take(arrived.reshape(block, rows, SPEC), slot_order[0], axis=0)
-    own = arranged.transpose(1, 0, 2).reshape(rows // 2, 2 * block, SPEC)
-    return correlate(n, own)
+    rows, columns = 2 * CH // groups, groups // 4
+    plane = [[f for f in range(groups) if f // 2 % 2 == z] for z in range(2)]
+    leaving = quantized.reshape(inputs, columns, 2, 2, rows, SPEC).transpose(1, 3, 2, 0, 4, 5)
+    arrived = lax.all_to_all(
+        leaving.reshape(2 * columns, 2 * inputs * rows, SPEC), "freq", 0, 0, axis_index_groups=plane, tiled=True)
+    held = 2 * columns * inputs
+    halves = arrived.reshape(2 * columns, 2, inputs, rows, SPEC).transpose(1, 3, 0, 2, 4)
+    halves = halves.reshape(2, rows // 2, 2 * held, SPEC)
+    z = lax.axis_index("freq") // 2 % 2
+    keep = lax.dynamic_index_in_dim(halves, z, 0, keepdims=False)
+    swap = lax.dynamic_index_in_dim(halves, 1 - z, 0, keepdims=False)
+    wanted = slot_order[0]
+    chip = 2 * inputs
+    inside = wanted // (2 * chip) * chip + wanted % chip
+    onehot = inside[:, None] == jnp.arange(held)[None, :]
+    here = (wanted // chip % 2 == z)[:, None]
+    return correlate(
+        n, keep, swap, (onehot & here).astype(jnp.bfloat16), (onehot & ~here).astype(jnp.bfloat16))
 
 
 def solution(mesh):

time: 207 us -> 210 us (1.014)
  Pallas kernels: 136 us -> 164 us
  waiting for transfers between devices: 32.1 us -> 16.9 us
  starting transfers between devices: 22.2 us -> 10.4 us
  local copies, waits for them, and re-layouts: 5.69 us -> 9.33 us
    pallas_call x1, Pallas kernels: 136 us -> 164 us  [correlate(): pl.pallas_call(functools.partial(correlate_kernel, n), out_shape=jax.Shap...]
    all_to_all x1, waiting for transfers between devices: 32.1 us -> 16.9 us  [body(): lax.all_to_all(leaving.reshape(2 * columns, 2 * inputs * rows, SPEC), 'fr...]
    all_to_all x1, starting transfers between devices: 22.2 us -> 10.4 us  [body(): lax.all_to_all(leaving.reshape(2 * columns, 2 * inputs * rows, SPEC), 'fr...]
    dynamic_slice x0 -> x1, local copies, waits for them, and re-layouts: none -> 2.17 us  [body(): swap = lax.dynamic_index_in_dim(halves, 1 - z, 0, keepdims=False)]
where the time goes in v3:
time: 210 us; the launch traced here: 209 us
  Pallas kernels  164 us (78%)
  waiting for transfers between devices  16.9 us (8%)
  starting transfers between devices  10.4 us (5%)
  local copies, waits for them, and re-layouts  9.33 us (4%)
  matrix products  4.63 us (2%)
  other arithmetic  3.59 us (2%)
    pallas_call x1, Pallas kernels, correlate(): pl.pallas_call(functools.partial(correlate_kernel, n), out_shape=jax.Shap...  164 us
    all_to_all x1, waiting for transfers between devices, body(): lax.all_to_all(leaving.reshape(2 * columns, 2 * inputs * rows, SPEC), 'fr...  16.9 us
    all_to_all x1, starting transfers between devices, body(): lax.all_to_all(leaving.reshape(2 * columns, 2 * inputs * rows, SPEC), 'fr...  10.4 us
    dot_general x1, matrix products, body(): jnp.einsum('kn,isn->iks', table, fir, preferred_element_type=jnp.float32)  4.63 us
  transfers between devices with their start and end apart: 1, of which 1 were waited for; matrix products, arithmetic and copies ran while one was open for 0% of the time, Pallas kernels for 0%

profile of v3, /device:TPU:1, one launch (start us, length us, event | category | flops | bytes accessed | tf_op | source)
XLA Modules:
  0.0 209.3 jit_solution(17521120207804868600)
XLA Ops:
  0.0 0.0 copy-start
  0.0 0.1 fusion.15
  0.1 2.2 %negate_convert_fusion = (bf16[256,1,512]{2,0,1:T(8,128)(2,1)S(1)}, bf16[256,1,512]{2,0,1:T(8,128)(2,1)S(1)}) fusion(), kind=kLoop, calls=%fused_computation.13 | loop fusion | flops 2228224 | bytes 524288 | tf_op jit(solution)/shard_map/convert.1
  2.3 0.7 subtract_convert_fusion
  3.0 0.1 pad_maximum_fusion
  3.0 0.5 copy.11
  3.6 1.0 reshape.226
  4.6 0.0 copy-done
  4.6 0.6 reshape.220
  5.2 4.6 %multiply_reduce_fusion = (f32[2,512]{1,0:T(2,128)S(1)}, f32[2,512,512]{1,2,0:T(8,128)S(1)}) fusion(bf16[512,512,1]{1,0,2:T(8,128)(2,1)} %reshape.226, bf16[2,523,512]{2,1,0:T(8,128)(2,1)S(1)} %reshape.220, f32[512]{0:T(512)S(1)} %get-tuple-element.10, f32[512]{0:T(512)S(1)} %get-tuple-element.11, f32[512]{0:T(512)S(1)} %get-tuple-element.12, ...), kind=kOutput, calls=%fused_computation.1 | convolution fusion | flops 556792832 | bytes 15233024 | tf_op jit(solution)/shard_map/kn,isn->iks/dot_general | solution.py:218
  9.9 0.2 reshape.221
  10.1 0.1 reduce_sum.19
  10.2 0.1 rsqrt_multiply_fusion
  10.3 0.1 broadcast_in_dim.7
  10.4 0.2 mul.536
  10.6 0.2 multiply_convert_fusion
  10.8 0.0 copy-start.1
  10.9 1.1 copy.12
  12.0 10.4 %all-to-all-start = ((bf16[32,32,512]{2,1,0:T(8,128)(2,1)}), bf16[32,32,512]{2,1,0:T(8,128)(2,1)S(1)}, u32[]{:S(2)}, u32[]{:S(2)}) async-start(bf16[32,32,512]{2,1,0:T(8,128)(2,1)} %bitcast.3), calls=%async_computation | async-start | bytes 2097152 | tf_op jit(solution)/shard_map/all_to_all | solution.py:228
  22.4 0.0 copy-done.1
  22.5 0.1 fusion.10
  22.6 16.9 %all-to-all-done = bf16[32,32,512]{2,1,0:T(8,128)(2,1)S(1)} async-done(((bf16[32,32,512]{2,1,0:T(8,128)(2,1)}), bf16[32,32,512]{2,1,0:T(8,128)(2,1)S(1)}, u32[]{:S(2)}, u32[]{:S(2)}) %all-to-all-start) | async-done | bytes 1048608 | tf_op jit(solution)/shard_map/all_to_all | solution.py:228
  39.5 1.1 copy.13
  40.6 2.2 %constant_dynamic-slice_fusion = (bf16[1,4,128,512]{3,0,2,1:T(2,128)(2,1)S(1)}, bf16[1,4,128,512]{3,0,2,1:T(2,128)(2,1)S(1)}) fusion(bf16[2,4,128,512]{3,0,2,1:T(2,128)(2,1)S(1)} %bitcast.38, s32[]{:T(128)S(6)} %select_n.218, s32[]{:T(128)S(6)} %select_n.217), kind=kLoop, calls=%fused_computation.65 | loop fusion | bytes 2097160 | tf_op jit(solution)/shard_map/jit(dynamic_index_in_dim)/dynamic_slice | solution.py:235
  42.8 0.1 copy.18
  42.9 0.1 copy.19
  43.1 164.2 %shard_map.37 = f32[4,2,128,1024]{3,2,1,0:T(8,128)S(1)} custom-call(bf16[4,128,512]{2,1,0:T(8,128)(2,1)S(1)} %bitcast.37, bf16[4,128,512]{2,1,0:T(8,128)(2,1)S(1)} %bitcast.36, bf16[128,64]{1,0:T(8,128)(2,1)S(1)} %get-tuple-element.22.place_keep, bf16[128,64]{1,0:T(8,128)(2,1)S(1)} %get-tuple-element.21.place_swap), custom_call_target="tpu_custom_call" | custom-call | tf_op jit(solution)/shard_map/pallas_call | solution.py:194
  207.3 2.0 copy.21
  (3 shorter events, 0.0 us)
Async XLA Ops:
  0.0 4.6 %copy-start = (bf16[2,267776]{1,0:T(2,128)(2,1)S(1)}, bf16[2,267776]{1,0:T(2,128)(2,1)}, u32[]{:S(2)}) copy-start(bf16[2,267776]{1,0:T(2,128)(2,1)} %param.3) | copy-start | bytes 3213316
  10.8 11.6 %copy-start.1 = (s32[1,128]{1,0:T(1,128)S(1)}, s32[1,128]{1,0:T(1,128)}, u32[]{:S(2)}) copy-start(s32[1,128]{1,0:T(1,128)} %param.4) | copy-start | bytes 1540
  12.0 27.6 %all-to-all-start = ((bf16[32,32,512]{2,1,0:T(8,128)(2,1)}), bf16[32,32,512]{2,1,0:T(8,128)(2,1)S(1)}, u32[]{:S(2)}, u32[]{:S(2)}) async-start(bf16[32,32,512]{2,1,0:T(8,128)(2,1)} %bitcast.3), calls=%async_computation | async-start | bytes 2097152 | tf_op jit(solution)/shard_map/all_to_all | solution.py:228

commit v4 on v3

--- a/solution.py
+++ b/solution.py
@@ -3,6 +3,8 @@
 
 import jax
 import jax.numpy as jnp
+import ml_dtypes
+import numpy as np
 from jax import lax
 from jax.experimental import pallas as pl
 from jax.experimental.pallas import tpu as pltpu
@@ -25,11 +27,9 @@
 
 def twiddle():
     frame = 2 * CH
-    chan = jnp.arange(CH, dtype=jnp.int32)[:, None]
-    point = jnp.arange(frame, dtype=jnp.int32)[None, :]
-    phase = (chan * point % frame).astype(jnp.float32) * (2.0 * math.pi / frame)
-    table = jnp.stack([jnp.cos(phase), -jnp.sin(phase)], axis=1)
-    return table.reshape(2 * CH, frame).astype(jnp.bfloat16)
+    phase = np.arange(CH)[:, None] * np.arange(frame)[None, :] % frame * (2.0 * math.pi / frame)
+    table = np.stack([np.cos(phase), -np.sin(phase)], axis=1)
+    return table.reshape(2 * CH, frame).astype(np.float32).astype(ml_dtypes.bfloat16)
 
 
 def tile(rows, cols):
@@ -40,7 +40,7 @@
     return real * (1.0 / SPEC), imag * (1.0 / SPEC)
 
 
-def correlate_kernel(n, keep, swap, place_keep, place_swap, out, own, xbuf, xsend, xrecv, nbuf, fbuf, ts, tr, nsend, nrecv, frecv, tsend, trecv):
+def correlate_kernel(n, halves, place_keep, place_swap, out, own, xbuf, xsend, xrecv, nbuf, fbuf, ts, tr, nsend, nrecv, frecv, tsend, trecv):
     me = lax.axis_index("blk")
     half, chans, block = n // 2, own.shape[0], own.shape[1] // 2
     mid = half - 1
@@ -83,11 +83,12 @@
         give(t, v, slot, c).start()
 
     group = lax.axis_index("freq")
-    partner = {"freq": group + 2 - 4 * lax.rem(group // 2, 2)}
+    z = lax.rem(group // 2, 2)
+    partner = {"freq": group + 2 - 4 * z}
 
     def exchange(c):
         return pltpu.make_async_remote_copy(
-            swap.at[c], xbuf.at[c], xsend.at[c], xrecv.at[c], device_id=partner, device_id_type=MESH)
+            halves.at[1 - z, c], xbuf.at[c], xsend.at[c], xrecv.at[c], device_id=partner, device_id_type=MESH)
 
     barrier = pltpu.get_barrier_semaphore()
     for k in range(1, n):
@@ -103,7 +104,7 @@
         exchange(c).wait_recv()
         for p in range(2):
             rows = pl.ds(p * (block // 2), block // 2)
-            mixed = jnp.dot(place_keep[...], keep[c, rows, :], preferred_element_type=jnp.float32)
+            mixed = jnp.dot(place_keep[...], halves[z, c, rows, :], preferred_element_type=jnp.float32)
             mixed += jnp.dot(place_swap[...], xbuf[c, rows, :], preferred_element_type=jnp.float32)
             own[c, pl.ds(p * block, block), :] = mixed.astype(jnp.bfloat16)
         start(0, c, own.at[c])
@@ -133,7 +134,9 @@
             @pl.when(place == mid)
             def _():
                 @pl.loop(0, mid)
-                def _(r):
+                def _(k):
+                    r = mid - 1 - k
+
                     @pl.when(r <= t)
                     def _():
                         relay(r, 1 + t, half + t, c, nbuf[r, c], fbuf[t, c])
@@ -182,8 +185,8 @@
                     give(t, v, 0, c).wait_send()
 
 
-def correlate(n, keep, swap, place_keep, place_swap):
-    chans, block, spec = keep.shape
+def correlate(n, halves, place_keep, place_swap):
+    _, chans, block, spec = halves.shape
     half, rows = n // 2, 2 * block
     own = pltpu.VMEM((chans, rows, spec), jnp.bfloat16)
     near = pltpu.VMEM((half - 1, chans, rows, spec), jnp.bfloat16)
@@ -194,21 +197,21 @@
     return pl.pallas_call(
         functools.partial(correlate_kernel, n),
         out_shape=jax.ShapeDtypeStruct((chans, 2, block, n * block), jnp.float32),
-        in_specs=[pl.BlockSpec(memory_space=pltpu.VMEM)] * 4,
+        in_specs=[pl.BlockSpec(memory_space=pltpu.VMEM)] * 3,
         out_specs=pl.BlockSpec(memory_space=pltpu.VMEM),
         scratch_shapes=[
-            own, pltpu.VMEM(keep.shape, jnp.bfloat16), dma((chans,)), dma((chans,)),
+            own, pltpu.VMEM(halves.shape[1:], jnp.bfloat16), dma((chans,)), dma((chans,)),
             near, far, leaving, arriving, dma((half, chans)), dma((half - 1, chans)), dma((half, chans)),
             dma((half - 1, half + 1, chans)), dma((n, chans))],
         compiler_params=pltpu.CompilerParams(
             collective_id=0, has_side_effects=True, vmem_limit_bytes=48 << 20),
-    )(keep, swap, place_keep, place_swap)
+    )(halves, place_keep, place_swap)
 
 
 def body(n, samples, slot_order, flags):
     inputs = samples.shape[0]
     taps = prototype()
-    table = twiddle()
+    table = jnp.asarray(twiddle())
     good = (1 - flags).astype(jnp.float32)
     frames = samples.reshape(inputs, SPEC + TAPS - 1, 2 * CH)
     total = jnp.zeros((inputs, SPEC, 2 * CH), jnp.float32)
@@ -231,15 +234,13 @@
     halves = arrived.reshape(2 * columns, 2, inputs, rows, SPEC).transpose(1, 3, 0, 2, 4)
     halves = halves.reshape(2, rows // 2, 2 * held, SPEC)
     z = lax.axis_index("freq") // 2 % 2
-    keep = lax.dynamic_index_in_dim(halves, z, 0, keepdims=False)
-    swap = lax.dynamic_index_in_dim(halves, 1 - z, 0, keepdims=False)
     wanted = slot_order[0]
     chip = 2 * inputs
     inside = wanted // (2 * chip) * chip + wanted % chip
     onehot = inside[:, None] == jnp.arange(held)[None, :]
     here = (wanted // chip % 2 == z)[:, None]
     return correlate(
-        n, keep, swap, (onehot & here).astype(jnp.bfloat16), (onehot & ~here).astype(jnp.bfloat16))
+        n, halves, (onehot & here).astype(jnp.bfloat16), (onehot & ~here).astype(jnp.bfloat16))
 
 
 def solution(mesh):

time: 210 us -> 203 us (0.967)
  Pallas kernels: 164 us -> 161 us
  local copies, waits for them, and re-layouts: 9.33 us -> 6.98 us
  other arithmetic: 3.59 us -> 1.36 us
    pallas_call x1, Pallas kernels: 164 us -> 161 us  [correlate(): pl.pallas_call(functools.partial(correlate_kernel, n), out_shape=jax.Shap...]
    another operation x2 -> x0, other arithmetic: 2.23 us -> none
    dynamic_slice x1 -> x0, local copies, waits for them, and re-layouts: 2.17 us -> none  [body(): swap = lax.dynamic_index_in_dim(halves, 1 - z, 0, keepdims=False)]
where the time goes in v4:
time: 203 us; the launch traced here: 202 us
  Pallas kernels  161 us (79%)
  waiting for transfers between devices  17 us (8%)
  starting transfers between devices  10.4 us (5%)
  local copies, waits for them, and re-layouts  6.98 us (3%)
  matrix products  4.63 us (2%)
    pallas_call x1, Pallas kernels, correlate(): pl.pallas_call(functools.partial(correlate_kernel, n), out_shape=jax.Shap...  161 us
    all_to_all x1, waiting for transfers between devices, body(): lax.all_to_all(leaving.reshape(2 * columns, 2 * inputs * rows, SPEC), 'fr...  17 us
    all_to_all x1, starting transfers between devices, body(): lax.all_to_all(leaving.reshape(2 * columns, 2 * inputs * rows, SPEC), 'fr...  10.4 us
    dot_general x1, matrix products, body(): jnp.einsum('kn,isn->iks', table, fir, preferred_element_type=jnp.float32)  4.63 us
  transfers between devices with their start and end apart: 1, of which 1 were waited for; matrix products, arithmetic and copies ran while one was open for 0% of the time, Pallas kernels for 0%

profile of v4, /device:TPU:1, one launch (start us, length us, event | category | flops | bytes accessed | tf_op | source)
XLA Modules:
  0.0 201.9 jit_solution(7805156529800414756)
XLA Ops:
  0.0 0.1 fusion.9
  0.1 0.7 subtract_convert_fusion
  0.8 1.9 reshape.149
  2.7 4.6 %multiply_reduce_fusion = (f32[2,512]{1,0:T(2,128)S(1)}, f32[2,512,512]{1,2,0:T(8,128)S(1)}) fusion(bf16[512,512,1]{1,0,2:T(8,128)(2,1)} %constant.133, bf16[2,523,512]{2,1,0:T(8,128)(2,1)S(1)} %reshape.149, f32[512]{0:T(512)S(1)} %get-tuple-element.8, f32[512]{0:T(512)S(1)} %get-tuple-element.9, f32[512]{0:T(512)S(1)} %get-tuple-element.10, ...), kind=kOutput, calls=%fused_computation.1 | convolution fusion | flops 556792832 | bytes 15233024 | tf_op jit(solution)/shard_map/kn,isn->iks/dot_general | solution.py:221
  7.3 0.2 reshape.150
  7.5 0.1 reduce_sum.19
  7.7 0.1 rsqrt_multiply_fusion
  7.8 0.1 broadcast_in_dim.12
  7.9 0.2 mul.482
  8.1 0.2 multiply_convert_fusion
  8.3 0.0 copy-start
  8.3 1.1 copy.5
  9.4 10.4 %all-to-all-start = ((bf16[32,32,512]{2,1,0:T(8,128)(2,1)}), bf16[32,32,512]{2,1,0:T(8,128)(2,1)S(1)}, u32[]{:S(2)}, u32[]{:S(2)}) async-start(bf16[32,32,512]{2,1,0:T(8,128)(2,1)} %bitcast.4), calls=%async_computation | async-start | bytes 2097152 | tf_op jit(solution)/shard_map/all_to_all | solution.py:231
  19.9 0.0 copy-done
  19.9 0.1 fusion.4
  20.0 17.0 %all-to-all-done = bf16[32,32,512]{2,1,0:T(8,128)(2,1)S(1)} async-done(((bf16[32,32,512]{2,1,0:T(8,128)(2,1)}), bf16[32,32,512]{2,1,0:T(8,128)(2,1)S(1)}, u32[]{:S(2)}, u32[]{:S(2)}) %all-to-all-start) | async-done | bytes 1048608 | tf_op jit(solution)/shard_map/all_to_all | solution.py:231
  37.0 1.0 copy.6
  38.0 0.4 reshape.154.halves
  38.5 161.4 %shard_map.46 = f32[4,2,128,1024]{3,2,1,0:T(8,128)S(1)} custom-call(bf16[2,4,128,512]{3,2,1,0:T(8,128)(2,1)S(1)} %reshape.154.halves, bf16[128,64]{1,0:T(8,128)(2,1)S(1)} %get-tuple-element.20.place_keep, bf16[128,64]{1,0:T(8,128)(2,1)S(1)} %get-tuple-element.19.place_swap), custom_call_target="tpu_custom_call" | custom-call | tf_op jit(solution)/shard_map/pallas_call | solution.py:197
  199.9 2.0 copy.8
  (3 shorter events, 0.0 us)
Async XLA Ops:
  8.3 11.6 %copy-start = (s32[1,128]{1,0:T(1,128)S(1)}, s32[1,128]{1,0:T(1,128)}, u32[]{:S(2)}) copy-start(s32[1,128]{1,0:T(1,128)} %param.5) | copy-start | bytes 1540
  9.4 27.6 %all-to-all-start = ((bf16[32,32,512]{2,1,0:T(8,128)(2,1)}), bf16[32,32,512]{2,1,0:T(8,128)(2,1)S(1)}, u32[]{:S(2)}, u32[]{:S(2)}) async-start(bf16[32,32,512]{2,1,0:T(8,128)(2,1)} %bitcast.4), calls=%async_computation | async-start | bytes 2097152 | tf_op jit(solution)/shard_map/all_to_all | solution.py:231

commit v5 on v4

--- a/solution.py
+++ b/solution.py
@@ -231,12 +231,13 @@
     arrived = lax.all_to_all(
         leaving.reshape(2 * columns, 2 * inputs * rows, SPEC), "freq", 0, 0, axis_index_groups=plane, tiled=True)
     held = 2 * columns * inputs
-    halves = arrived.reshape(2 * columns, 2, inputs, rows, SPEC).transpose(1, 3, 0, 2, 4)
+    halves = arrived.reshape(2 * columns, 2, inputs, rows, SPEC).transpose(1, 3, 2, 0, 4)
     halves = halves.reshape(2, rows // 2, 2 * held, SPEC)
     z = lax.axis_index("freq") // 2 % 2
     wanted = slot_order[0]
     chip = 2 * inputs
-    inside = wanted // (2 * chip) * chip + wanted % chip
+    source = wanted // (2 * chip) * 2 + wanted % chip // inputs
+    inside = wanted % inputs * (2 * columns) + source
     onehot = inside[:, None] == jnp.arange(held)[None, :]
     here = (wanted // chip % 2 == z)[:, None]
     return correlate(

time: 203 us -> 202 us (level)
  no operation moved by 1% of the time
where the time goes in v5:
time: 202 us; the launch traced here: 201 us
  Pallas kernels  161 us (80%)
  waiting for transfers between devices  17 us (8%)
  starting transfers between devices  10.4 us (5%)
  local copies, waits for them, and re-layouts  6.11 us (3%)
  matrix products  4.63 us (2%)
    pallas_call x1, Pallas kernels, correlate(): pl.pallas_call(functools.partial(correlate_kernel, n), out_shape=jax.Shap...  161 us
    all_to_all x1, waiting for transfers between devices, body(): lax.all_to_all(leaving.reshape(2 * columns, 2 * inputs * rows, SPEC), 'fr...  17 us
    all_to_all x1, starting transfers between devices, body(): lax.all_to_all(leaving.reshape(2 * columns, 2 * inputs * rows, SPEC), 'fr...  10.4 us
    dot_general x1, matrix products, body(): jnp.einsum('kn,isn->iks', table, fir, preferred_element_type=jnp.float32)  4.63 us
  transfers between devices with their start and end apart: 1, of which 1 were waited for; matrix products, arithmetic and copies ran while one was open for 0% of the time, Pallas kernels for 0%

profile of v5, /device:TPU:1, one launch (start us, length us, event | category | flops | bytes accessed | tf_op | source)
XLA Modules:
  0.0 201.0 jit_solution(7103163573768174719)
XLA Ops:
  0.0 0.1 fusion.9
  0.1 0.7 subtract_convert_fusion
  0.8 1.9 reshape.186
  2.7 4.6 %multiply_reduce_fusion = (f32[2,512]{1,0:T(2,128)S(1)}, f32[2,512,512]{1,2,0:T(8,128)S(1)}) fusion(bf16[512,512,1]{1,0,2:T(8,128)(2,1)} %constant.147, bf16[2,523,512]{2,1,0:T(8,128)(2,1)S(1)} %reshape.186, f32[512]{0:T(512)S(1)} %get-tuple-element.8, f32[512]{0:T(512)S(1)} %get-tuple-element.9, f32[512]{0:T(512)S(1)} %get-tuple-element.10, ...), kind=kOutput, calls=%fused_computation.1 | convolution fusion | flops 556792832 | bytes 15233024 | tf_op jit(solution)/shard_map/kn,isn->iks/dot_general | solution.py:221
  7.3 0.2 reshape.187
  7.5 0.1 reduce_sum.19
  7.7 0.1 rsqrt_multiply_fusion
  7.8 0.1 broadcast_in_dim.12
  7.9 0.2 mul.490
  8.1 0.2 multiply_convert_fusion
  8.3 0.0 copy-start
  8.3 1.1 copy.5
  9.4 10.4 %all-to-all-start = ((bf16[32,32,512]{2,1,0:T(8,128)(2,1)}), bf16[32,32,512]{2,1,0:T(8,128)(2,1)S(1)}, u32[]{:S(2)}, u32[]{:S(2)}) async-start(bf16[32,32,512]{2,1,0:T(8,128)(2,1)} %bitcast.4), calls=%async_computation | async-start | bytes 2097152 | tf_op jit(solution)/shard_map/all_to_all | solution.py:231
  19.9 0.0 copy-done
  19.9 0.1 fusion.4
  20.0 17.0 %all-to-all-done = bf16[32,32,512]{2,1,0:T(8,128)(2,1)S(1)} async-done(((bf16[32,32,512]{2,1,0:T(8,128)(2,1)}), bf16[32,32,512]{2,1,0:T(8,128)(2,1)S(1)}, u32[]{:S(2)}, u32[]{:S(2)}) %all-to-all-start) | async-done | bytes 1048608 | tf_op jit(solution)/shard_map/all_to_all | solution.py:231
  37.0 0.6 copy.6
  37.6 161.4 %shard_map.46 = f32[4,2,128,1024]{3,2,1,0:T(8,128)S(1)} custom-call(bf16[2,4,128,512]{3,2,1,0:T(8,128)(2,1)S(1)} %bitcast.31, bf16[128,64]{1,0:T(8,128)(2,1)S(1)} %get-tuple-element.20.place_keep, bf16[128,64]{1,0:T(8,128)(2,1)S(1)} %get-tuple-element.19.place_swap), custom_call_target="tpu_custom_call" | custom-call | tf_op jit(solution)/shard_map/pallas_call | solution.py:197
  199.0 2.0 %copy.8 = f32[4,2,128,1024]{3,2,1,0:T(8,128)} copy(f32[4,2,128,1024]{3,2,1,0:T(8,128)S(1)} %shard_map.46) | data formatting | bytes 8388608
  (3 shorter events, 0.0 us)
Async XLA Ops:
  8.3 11.6 %copy-start = (s32[1,128]{1,0:T(1,128)S(1)}, s32[1,128]{1,0:T(1,128)}, u32[]{:S(2)}) copy-start(s32[1,128]{1,0:T(1,128)} %param.5) | copy-start | bytes 1540
  9.4 27.6 %all-to-all-start = ((bf16[32,32,512]{2,1,0:T(8,128)(2,1)}), bf16[32,32,512]{2,1,0:T(8,128)(2,1)S(1)}, u32[]{:S(2)}, u32[]{:S(2)}) async-start(bf16[32,32,512]{2,1,0:T(8,128)(2,1)} %bitcast.4), calls=%async_computation | async-start | bytes 2097152 | tf_op jit(solution)/shard_map/all_to_all | solution.py:231
